TPU v7x, 512 devices: a whole 4x8x8 slice. The times are simulated.
512 devices in a mesh: ab: 16 (over y, x_lo), cd: 32 (over z, x_hi, core).
Axes of the slice: x: 4 (x_hi: 2, x_lo: 2; x = x_hi * 2 + x_lo), y: 8, z: 8, core: 2. Of those that a mesh axis runs over, the one named last changes fastest.
Arguments:
- factors: bfloat16 [128, 128, 2048], P('ab', 'cd'), may hold values from -0.25 to 0.25
- amplitudes: float32 [256, 128, 128], P('cd', 'ab'), may hold values from -4 to 4
- driving: float32 [256, 128, 128], P('cd', 'ab'), may hold values from -8 to 8
- occ_energy: float32 [32], replicated, may hold values from -2 to -0.5
- vir_energy: float32 [128], replicated, may hold values from 0.5 to 3
Outputs:
- new_amplitudes: float32 [256, 128, 128], P('cd', 'ab')
- residual: float32 [256, 128, 128], P('cd', 'ab')
All inputs are finite; a program needn't handle non-finite values.
Results may differ from a plain program's by a relative error of at most 0.0036.
Values may be sent and summed in bfloat16 or wider, within the bound.
No kernel may reach another device: no remote copies, remote signals or barrier semaphores. Data moves between devices by JAX's collectives and lax.ppermute only.
A program may use at most 64 MiB of HBM per device.

v0:
```python
import jax
import jax.numpy as jnp
from jax import lax
from jax.sharding import PartitionSpec as P

ITERS = 2


def local(factors, amplitudes, driving, occ_energy, vir_energy):
    rows = amplitudes.shape[0]
    a_local = amplitudes.shape[1]
    virtuals = amplitudes.shape[2]
    aux_width = factors.shape[2]
    n_cd = lax.axis_size("cd")
    d_local = factors.shape[1]
    pairs = rows * n_cd
    cd_index = lax.axis_index("cd")
    ab_index = lax.axis_index("ab")
    left_rows = lax.all_gather(factors, "cd", axis=1, tiled=True)
    left_flat = left_rows.reshape(a_local * virtuals, aux_width)
    piece = lax.all_gather(factors, "ab", axis=0, tiled=True)
    count = piece.shape[0]
    product = lax.dot_general(
        left_flat,
        piece.reshape(count * d_local, aux_width),
        (((1,), (1,)), ((), ())),
        preferred_element_type=jnp.float32,
    )
    product = product.reshape(a_local, virtuals, count, d_local)
    tiles = (
        product.transpose(0, 2, 3, 1)
        .reshape(a_local, count, d_local * virtuals)
        .astype(jnp.bfloat16)
    )
    tiles = tiles.reshape(a_local * virtuals, d_local * virtuals)
    n_occ = occ_energy.shape[0]
    row_ids = cd_index * rows + lax.iota(jnp.int32, rows)
    orbitals = lax.iota(jnp.int32, n_occ)
    first_hot = (row_ids[:, None] // n_occ == orbitals[None, :]).astype(jnp.float32)
    second_hot = (row_ids[:, None] % n_occ == orbitals[None, :]).astype(jnp.float32)
    occ_pair = jnp.sum((first_hot + second_hot) * occ_energy[None, :], axis=1)
    vir_rows = lax.dynamic_slice_in_dim(vir_energy, ab_index * a_local, a_local)
    denominator = vir_rows[None, :, None] + vir_energy[None, None, :] - occ_pair[:, None, None]
    current = amplitudes
    residual = amplitudes
    for step in range(ITERS):
        rounded = current.astype(jnp.bfloat16)
        every_row = lax.all_gather(rounded, "cd", axis=0, tiled=True)
        columns = lax.dynamic_slice_in_dim(every_row, cd_index * d_local, d_local, 2)
        own_block = columns.transpose(2, 1, 0)
        gathered = lax.all_gather(own_block, "ab", axis=1, tiled=True)
        flat_amps = gathered.reshape(d_local * virtuals, pairs)
        summed = lax.psum_scatter(
            lax.dot_general(
                flat_amps, tiles, (((0,), (1,)), ((), ())), preferred_element_type=jnp.float32
            ),
            "cd",
            scatter_dimension=0,
            tiled=True,
        ).reshape(rows, a_local, virtuals)
        mirrored = lax.all_to_all(summed, "ab", split_axis=2, concat_axis=1, tiled=True).transpose(
            0, 2, 1
        )
        symmetric = 0.5 * (summed + mirrored)
        residual = driving + denominator * current + symmetric
        current = current - residual / denominator
    return (current, residual)


def solution(mesh):
    placed = (P("ab", "cd", None), P("cd", "ab", None), P("cd", "ab", None), P(), P())
    return jax.shard_map(
        local,
        mesh=mesh,
        in_specs=placed,
        out_specs=(P("cd", "ab", None), P("cd", "ab", None)),
        check_vma=False,
    )
```

profile of v0, /device:TPU:4, one launch (start us, length us, event | category | flops | bytes accessed | tf_op | source)
XLA Modules:
  0.0 559.9 jit_solution(14078645966678964496)
XLA Ops:
  7.2 1.6 copy.37
  8.9 0.7 all-gather.3.cloned.1.call-update
  9.7 0.8 convert_element_type.25
  10.4 45.7 %all_gather.18 = bf16[256,8,128]{2,1,0:T(8,128)(2,1)S(1)} all-gather(bf16[8,8,128]{2,1,0:T(8,128)(2,1)S(1)} %convert_element_type.25), channel_id=1, replica_groups=mesh['ab'=16,'cd'=32] {'cd'}, dimensions={0}, use_global_device_ids=true | all-gather | bytes 540672 | tf_op jit(solution)/shard_map/all_gather | solution.py:48
  56.3 0.3 copy.57
  56.7 36.1 %all_gather.19 = bf16[4,128,256]{2,1,0:T(8,128)(2,1)S(1)} all-gather(bf16[4,8,256]{2,1,0:T(8,128)(2,1)S(1)} %bitcast.73), channel_id=1, replica_groups=mesh['ab'=16,'cd'=32] {'ab'}, dimensions={1}, use_global_device_ids=true | all-gather | bytes 278528 | tf_op jit(solution)/shard_map/all_gather | solution.py:51
  92.8 92.8 %all-gather.3.cloned.1.call-done = bf16[8,128,2048]{2,0,1:T(8,128)(2,1)} async-done(((bf16[8,4,2048]{2,0,1:T(8,128)(2,1)}), bf16[8,128,2048]{2,0,1:T(8,128)(2,1)}) %all-gather.3.cloned.1.call-update) | async-done | bytes 4194320 | tf_op jit(solution)/shard_map/all_gather | solution.py:19
  185.5 7.7 %fusion.8 = bf16[8,128,4,128]{1,3,2,0:T(8,128)(2,1)S(1)} fusion(bf16[128,4,2048]{2,0,1:T(8,128)(2,1)} %all-gather.5.cloned.1.call-done, bf16[8,128,2048,1]{2,0,1,3:T(8,128)(2,1)} %bitcast.75), kind=kOutput, calls=%fused_computation.4 | convolution fusion | flops 2148007936 | bytes 7340032 | tf_op jit(solution)/shard_map/dot_general | solution.py:23
  193.2 0.7 copy.40
  193.9 1.4 fusion.15
  195.6 122.6 %reduce-scatter.3.cloned.1.call-done = f32[8,1024]{1,0:T(8,128)} async-done(((f32[256,1024]{1,0:T(8,128)}), f32[8,1024]{1,0:T(8,128)}) %reduce-scatter.3.cloned.1.call-update) | async-done | bytes 32784 | tf_op jit(solution)/shard_map/reduce_scatter | solution.py:53
  318.1 1.0 copy.41
  319.1 0.9 reshape.124
  320.0 7.4 %all-to-all-start = ((f32[16,1,512]{2,1,0:T(1,128)}), f32[16,1,512]{2,1,0:T(1,128)S(1)}, u32[]{:S(2)}, u32[]{:S(2)}) async-start(f32[16,1,512]{2,1,0:T(1,128)} %reshape.124), calls=%async_computation.1 | async-start | bytes 65536 | tf_op jit(solution)/shard_map/all_to_all | solution.py:61
  327.6 8.5 %all-to-all-done = f32[16,1,512]{2,1,0:T(1,128)S(1)} async-done(((f32[16,1,512]{2,1,0:T(1,128)}), f32[16,1,512]{2,1,0:T(1,128)S(1)}, u32[]{:S(2)}, u32[]{:S(2)}) %all-to-all-start) | async-done | bytes 32800 | tf_op jit(solution)/shard_map/all_to_all | solution.py:61
  336.2 0.5 broadcast.123
  336.7 0.7 reduce
  337.4 0.3 reshape.125
  337.7 0.3 copy.43
  338.3 0.8 fusion.28
  339.2 38.9 %all_gather.22 = bf16[256,8,128]{2,1,0:T(8,128)(2,1)S(1)} all-gather(bf16[8,8,128]{2,1,0:T(8,128)(2,1)S(1)} %get-tuple-element.4), channel_id=1, replica_groups=mesh['ab'=16,'cd'=32] {'cd'}, dimensions={0}, use_global_device_ids=true | all-gather | bytes 540672 | tf_op jit(solution)/shard_map/all_gather | solution.py:48
  378.2 0.4 copy.58
  378.6 32.1 %all_gather.23 = bf16[4,128,256]{2,1,0:T(8,128)(2,1)S(1)} all-gather(bf16[4,8,256]{2,1,0:T(8,128)(2,1)S(1)} %bitcast.74), channel_id=1, replica_groups=mesh['ab'=16,'cd'=32] {'ab'}, dimensions={1}, use_global_device_ids=true | all-gather | bytes 278528 | tf_op jit(solution)/shard_map/all_gather | solution.py:51
  410.7 1.4 fusion.13
  412.1 120.8 %reduce-scatter.5.cloned.1.call-done = f32[8,1024]{1,0:T(8,128)} async-done(((f32[256,1024]{1,0:T(8,128)}), f32[8,1024]{1,0:T(8,128)}) %reduce-scatter.5.cloned.1.call-update) | async-done | bytes 32784 | tf_op jit(solution)/shard_map/reduce_scatter | solution.py:53
  532.9 1.0 copy.46
  533.9 0.3 reshape.126
  534.2 16.0 %all_to_all.36 = f32[16,1,512]{2,1,0:T(1,128)S(1)} all-to-all(f32[16,1,512]{2,1,0:T(1,128)S(1)} %reshape.126), channel_id=1, replica_groups=mesh['ab'=16,'cd'=32] {'ab'}, dimensions={0} | all-to-all | bytes 65536 | tf_op jit(solution)/shard_map/all_to_all | solution.py:61
  550.3 0.7 reduce.1
  551.0 0.3 reshape.127
  551.3 0.3 copy.48
  551.9 1.5 fusion.24
  (24 shorter events, 1.5 us)
Async XLA Ops:
  7.2 85.6 %all-gather.5.cloned.1.call-start = ((), (), s32[]{:S(2)}) async-start(), calls=%async_computation.5 | async-start | bytes 2228224 | tf_op jit(solution)/shard_map/all_gather | solution.py:21
  8.9 176.7 %all-gather.3.cloned.1.call-start = ((), (), s32[]{:S(2)}) async-start(), calls=%async_computation.4 | async-start | bytes 4325376 | tf_op jit(solution)/shard_map/all_gather | solution.py:19
  9.6 308.5 %reduce-scatter.3.cloned.1.call-start = ((), (), s32[]{:S(2)}) async-start(), calls=%async_computation.6 | async-start | bytes 1081344 | tf_op jit(solution)/shard_map/reduce_scatter | solution.py:53
  193.2 2.2 copy-start.2
  193.2 134.2 %copy-start.3 = (f32[32]{0:T(128)S(1)}, f32[32]{0:T(128)}, u32[]{:S(2)}) copy-start(f32[32]{0:T(128)} %param.8) | copy-start | bytes 388
  193.2 145.1 %copy-start = (f32[8,8,128]{2,1,0:T(8,128)S(1)}, f32[8,8,128]{2,1,0:T(8,128)}, u32[]{:S(2)}) copy-start(f32[8,8,128]{2,1,0:T(8,128)} %param.7) | copy-start | bytes 98308
  193.2 145.1 %copy-start.1 = (f32[8,8,128]{2,1,0:T(8,128)S(1)}, f32[8,8,128]{2,1,0:T(8,128)}, u32[]{:S(2)}) copy-start(f32[8,8,128]{2,1,0:T(8,128)} %param.6) | copy-start | bytes 98308
  320.0 16.1 %all-to-all-start = ((f32[16,1,512]{2,1,0:T(1,128)}), f32[16,1,512]{2,1,0:T(1,128)S(1)}, u32[]{:S(2)}, u32[]{:S(2)}) async-start(f32[16,1,512]{2,1,0:T(1,128)} %reshape.124), calls=%async_computation.1 | async-start | bytes 65536 | tf_op jit(solution)/shard_map/all_to_all | solution.py:61
  327.4 205.5 %reduce-scatter.5.cloned.1.call-start = ((), (), s32[]{:S(2)}) async-start(), calls=%async_computation.7 | async-start | bytes 1081344 | tf_op jit(solution)/shard_map/reduce_scatter | solution.py:53
Sparse Core Ops, SparseCore 0:
  10.1 82.6 all-gather.4
  96.1 89.3 all-gather.2
  195.5 122.5 reduce-scatter.2
  412.2 120.6 reduce-scatter.4
where the time goes:
time: 560 us
  waiting for transfers between devices  345 us (62%)
  blocking collectives  169 us (30%)
  between operations  13.9 us (2%)
  matrix products  10.5 us (2%)
  local copies, waits for them, and re-layouts  8.95 us (2%)
  starting transfers between devices  7.52 us (1%)
    reduce_scatter x2, waiting for transfers between devices, local(): lax.psum_scatter(lax.dot_general(flat_amps, tiles, (((0,), (1,)), ((), ()...  243 us
    all_gather x1, waiting for transfers between devices, local(): left_rows = lax.all_gather(factors, 'cd', axis=1, tiled=True)  92.8 us
    all_gather x2, blocking collectives, local(): every_row = lax.all_gather(rounded, 'cd', axis=0, tiled=True)  84.5 us
    all_gather x2, blocking collectives, local(): gathered = lax.all_gather(own_block, 'ab', axis=1, tiled=True)  68.2 us
    all_to_all x1, blocking collectives, local(): lax.all_to_all(summed, 'ab', split_axis=2, concat_axis=1, tiled=True)  16 us
  transfers between devices with their start and end apart: 5, of which 4 were waited for; matrix products, arithmetic and copies ran while one was open for 0% of the time, Pallas kernels for 0%

commit v1 on v0

--- a/solution.py
+++ b/solution.py
@@ -16,7 +16,14 @@
     pairs = rows * n_cd
     cd_index = lax.axis_index("cd")
     ab_index = lax.axis_index("ab")
-    left_rows = lax.all_gather(factors, "cd", axis=1, tiled=True)
+
+    def _switch_links(sample):
+        x_now = jnp.concatenate(
+            lax.all_to_all(jnp.stack(lax.axis_size("cd") * [sample], axis=0), "cd", 0, 0), axis=1
+        )
+        return x_now
+
+    left_rows = _switch_links(factors)
     left_flat = left_rows.reshape(a_local * virtuals, aux_width)
     piece = lax.all_gather(factors, "ab", axis=0, tiled=True)
     count = piece.shape[0]

time: 560 us -> 572 us (1.021)
  waiting for transfers between devices: 345 us -> 250 us
  blocking collectives: 169 us -> 247 us
  local copies, waits for them, and re-layouts: 8.95 us -> 27 us
  starting transfers between devices: 7.52 us -> 21.3 us
    all_gather x1 -> x0, waiting for transfers between devices: 92.8 us -> none  [local(): left_rows = lax.all_gather(factors, 'cd', axis=1, tiled=True)]
    all_gather x2, blocking collectives: 84.5 us -> 164 us  [local(): every_row = lax.all_gather(rounded, 'cd', axis=0, tiled=True)]
    all_to_all x0 -> x1, starting transfers between devices: none -> 13.6 us  [_switch_links(): lax.all_to_all(jnp.stack(lax.axis_size('cd') * [sample], axis=0), 'cd', 0...]
    reshape x0 -> x1, local copies, waits for them, and re-layouts: none -> 7.07 us  [_switch_links(): jnp.concatenate(lax.all_to_all(jnp.stack(lax.axis_size('cd') * [sample],...]
    dot_general x0 -> x1, local copies, waits for them, and re-layouts: none -> 6.88 us  [local(): lax.dot_general(left_flat, piece.reshape(count * d_local, aux_width), (((...]
  transfers between devices with their start and end apart: 5 -> 5, of which waited for: 4 -> 3; matrix products, arithmetic and copies ran while one was open for 0% -> 3% of each run, Pallas kernels for 0% -> 0%
where the time goes in v1:
time: 572 us
  waiting for transfers between devices  250 us (44%)
  blocking collectives  247 us (43%)
  local copies, waits for them, and re-layouts  27 us (5%)
  starting transfers between devices  21.3 us (4%)
  between operations  13.9 us (2%)
  matrix products  8.11 us (1%)
    reduce_scatter x2, waiting for transfers between devices, local(): lax.psum_scatter(lax.dot_general(flat_amps, tiles, (((0,), (1,)), ((), ()...  242 us
    all_gather x2, blocking collectives, local(): every_row = lax.all_gather(rounded, 'cd', axis=0, tiled=True)  164 us
    all_gather x2, blocking collectives, local(): gathered = lax.all_gather(own_block, 'ab', axis=1, tiled=True)  67.1 us
    all_to_all x1, blocking collectives, local(): lax.all_to_all(summed, 'ab', split_axis=2, concat_axis=1, tiled=True)  16 us
    all_to_all x1, starting transfers between devices, _switch_links(): lax.all_to_all(jnp.stack(lax.axis_size('cd') * [sample], axis=0), 'cd', 0...  13.6 us
  transfers between devices with their start and end apart: 5, of which 3 were waited for; matrix products, arithmetic and copies ran while one was open for 3% of the time, Pallas kernels for 0%

profile of v1, /device:TPU:4, one launch (start us, length us, event | category | flops | bytes accessed | tf_op | source)
XLA Modules:
  0.0 571.6 jit_solution(13106134802997649244)
XLA Ops:
  7.2 5.0 stack.2
  12.2 13.6 %all-to-all-start = ((bf16[32,8,4,2048]{3,2,1,0:T(4,128)(2,1)}), bf16[32,8,4,2048]{3,2,1,0:T(4,128)(2,1)}, u32[]{:S(2)}, u32[]{:S(2)}) async-start(bf16[32,8,4,2048]{3,2,1,0:T(4,128)(2,1)} %stack.2), calls=%async_computation | async-start | bytes 8388608 | tf_op jit(solution)/shard_map/all_to_all | solution.py:22
  25.9 0.7 copy.37
  26.7 125.4 %all_gather.15 = bf16[256,8,128]{2,1,0:T(8,128)(2,1)S(1)} all-gather(bf16[8,8,128]{2,1,0:T(8,128)(2,1)S(1)} %convert_element_type.25), channel_id=1, replica_groups=mesh['ab'=16,'cd'=32] {'cd'}, dimensions={0}, use_global_device_ids=true | all-gather | bytes 540672 | tf_op jit(solution)/shard_map/all_gather | solution.py:55
  152.3 0.3 copy.53
  152.6 35.0 %all_gather.16 = bf16[4,128,256]{2,1,0:T(8,128)(2,1)S(1)} all-gather(bf16[4,8,256]{2,1,0:T(8,128)(2,1)S(1)} %bitcast.80), channel_id=1, replica_groups=mesh['ab'=16,'cd'=32] {'ab'}, dimensions={1}, use_global_device_ids=true | all-gather | bytes 278528 | tf_op jit(solution)/shard_map/all_gather | solution.py:58
  187.7 7.1 %copy.36 = bf16[8,32,4,2048]{3,2,1,0:T(4,128)(2,1)} copy(bf16[8,32,4,2048]{3,2,0,1:T(4,128)(2,1)} %bitcast.2) | data formatting | bytes 8388608 | tf_op jit(solution)/shard_map/reshape | solution.py:21
  194.7 6.9 %reshape.127 = bf16[8,128,2048,1]{2,1,0,3:T(8,128)(2,1)} reshape(bf16[8,32,4,2048]{3,2,1,0:T(4,128)(2,1)} %copy.36) | data formatting | bytes 8388608 | tf_op jit(solution)/shard_map/dot_general | solution.py:30
  201.6 5.2 fusion.8
  206.9 0.7 copy.38
  207.6 1.4 fusion.15
  209.2 120.6 %reduce-scatter.3.cloned.1.call-done = f32[8,1024]{1,0:T(8,128)} async-done(((f32[256,1024]{1,0:T(8,128)}), f32[8,1024]{1,0:T(8,128)}) %reduce-scatter.3.cloned.1.call-update) | async-done | bytes 32784 | tf_op jit(solution)/shard_map/reduce_scatter | solution.py:60
  329.8 1.0 copy.39
  330.8 0.9 reshape.130
  331.7 7.5 %all-to-all-start.1 = ((f32[16,1,512]{2,1,0:T(1,128)}), f32[16,1,512]{2,1,0:T(1,128)S(1)}, u32[]{:S(2)}, u32[]{:S(2)}) async-start(f32[16,1,512]{2,1,0:T(1,128)} %reshape.130), calls=%async_computation.2 | async-start | bytes 65536 | tf_op jit(solution)/shard_map/all_to_all | solution.py:68
  339.5 8.5 %all-to-all-done.1 = f32[16,1,512]{2,1,0:T(1,128)S(1)} async-done(((f32[16,1,512]{2,1,0:T(1,128)}), f32[16,1,512]{2,1,0:T(1,128)S(1)}, u32[]{:S(2)}, u32[]{:S(2)}) %all-to-all-start.1) | async-done | bytes 32800 | tf_op jit(solution)/shard_map/all_to_all | solution.py:68
  348.1 0.5 broadcast.125
  348.6 0.7 reduce
  349.3 0.3 reshape.131
  349.6 0.3 copy.41
  350.2 0.8 fusion.28
  351.0 38.7 %all_gather.18 = bf16[256,8,128]{2,1,0:T(8,128)(2,1)S(1)} all-gather(bf16[8,8,128]{2,1,0:T(8,128)(2,1)S(1)} %get-tuple-element.4), channel_id=1, replica_groups=mesh['ab'=16,'cd'=32] {'cd'}, dimensions={0}, use_global_device_ids=true | all-gather | bytes 540672 | tf_op jit(solution)/shard_map/all_gather | solution.py:55
  389.9 0.4 copy.54
  390.3 32.1 %all_gather.19 = bf16[4,128,256]{2,1,0:T(8,128)(2,1)S(1)} all-gather(bf16[4,8,256]{2,1,0:T(8,128)(2,1)S(1)} %bitcast.81), channel_id=1, replica_groups=mesh['ab'=16,'cd'=32] {'ab'}, dimensions={1}, use_global_device_ids=true | all-gather | bytes 278528 | tf_op jit(solution)/shard_map/all_gather | solution.py:58
  422.4 1.4 fusion.13
  423.8 120.9 %reduce-scatter.5.cloned.1.call-done = f32[8,1024]{1,0:T(8,128)} async-done(((f32[256,1024]{1,0:T(8,128)}), f32[8,1024]{1,0:T(8,128)}) %reduce-scatter.5.cloned.1.call-update) | async-done | bytes 32784 | tf_op jit(solution)/shard_map/reduce_scatter | solution.py:60
  544.7 1.0 copy.44
  546.0 16.0 %all_to_all.41 = f32[16,1,512]{2,1,0:T(1,128)S(1)} all-to-all(f32[16,1,512]{2,1,0:T(1,128)S(1)} %reshape.132), channel_id=1, replica_groups=mesh['ab'=16,'cd'=32] {'ab'}, dimensions={0} | all-to-all | bytes 65536 | tf_op jit(solution)/shard_map/all_to_all | solution.py:68
  562.0 0.7 reduce.1
  562.8 0.3 reshape.133
  563.1 0.3 copy.46
  563.6 1.5 fusion.24
  (28 shorter events, 1.8 us)
Async XLA Ops:
  12.2 13.7 %copy-start = (bf16[8,4,2048]{2,1,0:T(4,128)(2,1)S(1)}, bf16[8,4,2048]{2,1,0:T(4,128)(2,1)}, u32[]{:S(2)}) copy-start(bf16[8,4,2048]{2,1,0:T(4,128)(2,1)} %param.5) | copy-start | bytes 393220
  12.2 14.5 %copy-start.2 = (f32[8,8,128]{2,1,0:T(8,128)S(1)}, f32[8,8,128]{2,1,0:T(8,128)}, u32[]{:S(2)}) copy-start(f32[8,8,128]{2,1,0:T(8,128)} %param.6) | copy-start | bytes 98308
  12.2 175.5 %all-to-all-start = ((bf16[32,8,4,2048]{3,2,1,0:T(4,128)(2,1)}), bf16[32,8,4,2048]{3,2,1,0:T(4,128)(2,1)}, u32[]{:S(2)}, u32[]{:S(2)}) async-start(bf16[32,8,4,2048]{3,2,1,0:T(4,128)(2,1)} %stack.2), calls=%async_computation | async-start | bytes 8388608 | tf_op jit(solution)/shard_map/all_to_all | solution.py:22
  25.8 175.8 %all-gather.2.cloned.1.call-start = ((), (), s32[]{:S(2)}) async-start(), calls=%async_computation.5 | async-start | bytes 2228224 | tf_op jit(solution)/shard_map/all_gather | solution.py:28
  26.6 303.2 %reduce-scatter.3.cloned.1.call-start = ((), (), s32[]{:S(2)}) async-start(), calls=%async_computation.6 | async-start | bytes 1081344 | tf_op jit(solution)/shard_map/reduce_scatter | solution.py:60
  206.8 2.2 copy-start.3
  206.8 132.5 %copy-start.4 = (f32[32]{0:T(128)S(1)}, f32[32]{0:T(128)}, u32[]{:S(2)}) copy-start(f32[32]{0:T(128)} %param.8) | copy-start | bytes 388
  206.9 143.3 %copy-start.1 = (f32[8,8,128]{2,1,0:T(8,128)S(1)}, f32[8,8,128]{2,1,0:T(8,128)}, u32[]{:S(2)}) copy-start(f32[8,8,128]{2,1,0:T(8,128)} %param.7) | copy-start | bytes 98308
  331.7 16.3 %all-to-all-start.1 = ((f32[16,1,512]{2,1,0:T(1,128)}), f32[16,1,512]{2,1,0:T(1,128)S(1)}, u32[]{:S(2)}, u32[]{:S(2)}) async-start(f32[16,1,512]{2,1,0:T(1,128)} %reshape.130), calls=%async_computation.2 | async-start | bytes 65536 | tf_op jit(solution)/shard_map/all_to_all | solution.py:68
  339.3 205.4 %reduce-scatter.5.cloned.1.call-start = ((), (), s32[]{:S(2)}) async-start(), calls=%async_computation.7 | async-start | bytes 1081344 | tf_op jit(solution)/shard_map/reduce_scatter | solution.py:60
Sparse Core Ops, SparseCore 0:
  28.7 104.9 all-gather.1
  209.2 120.6 reduce-scatter.2
  423.9 120.7 reduce-scatter.4
